TPU v7x, 32 devices: a whole 2x2x4 slice. The times are simulated.
32 devices in a mesh: row: 4 (over z), col: 8 (over y, x, core).
Axes of the slice: x: 2, y: 2, z: 4, core: 2. Of those that a mesh axis runs over, the one named last changes fastest.
Arguments:
- hamiltonian: bfloat16 [2048, 2048], P('row', 'col'), may hold values from -0.3 to 0.3
- pattern: int32 [16, 16], replicated, may hold values from 0 to 1, as said below
- tile_lists: int32 [32, 8], replicated, may hold values from 0 to 15, as said below
- orders: int32 [32], replicated, may hold values from 6 to 8
- shift: float32 [1], replicated, may hold values from -0.5 to 0.5
Outputs:
- density: bfloat16 [2048, 2048], P('row', 'col')
- php: float32 [2048, 2048], P('row', 'col')
Inputs may be any that keep to these rules, and one draw needn't show every extreme that they name: `pattern`: Symmetric, with zeros on the diagonal. `tile_lists`: row s begins with tile s * 64 // 128; its entries lie in distinct groups of 2 consecutive tiles, and the second lies in the group that shares a group of 4 consecutive tiles with the first. Entries from position orders[s] on are not used.
All inputs are finite; a program needn't handle non-finite values.
Results may differ from a plain program's by a relative error of at most 0.0073.
Values may be sent and summed in bfloat16 or wider, within the bound.
A program may use at most 64 MiB of HBM per device.

v0:
```python
import jax
import jax.numpy as jnp
from jax import lax
from jax.sharding import PartitionSpec as P

TILE = 128
TPC = 2
MAXT = 8
ITERS = 3


def newton_density(sub, live_rows, potential):
    eye = jnp.eye(sub.shape[0], dtype=jnp.float32)
    shifted = sub.astype(jnp.float32) - potential * eye * live_rows[None, :]
    row_squares = jnp.sum(shifted * shifted, axis=1)
    scale = jnp.abs(potential) + 2.0 * jnp.sqrt(jnp.max(row_squares) + 1e-06)
    iterate = (shifted / scale).astype(jnp.bfloat16)
    product = shifted
    for step in range(ITERS):
        square = jnp.dot(iterate, iterate, preferred_element_type=jnp.float32)
        factor = (1.5 * eye - 0.5 * square).astype(jnp.bfloat16)
        product = jnp.dot(iterate, factor, preferred_element_type=jnp.float32)
        if step + 1 < ITERS:
            iterate = product.astype(jnp.bfloat16)
    return 0.5 * (eye - product)


def per_device(hamiltonian, pattern, tile_lists, orders, shift):
    rows_n = lax.axis_size("row")
    cols_n = lax.axis_size("col")
    devices = rows_n * cols_n
    me_row = lax.axis_index("row")
    me_col = lax.axis_index("col")
    solver = me_row * cols_n + me_col
    count = pattern.shape[0]
    row_tiles = count // rows_n
    width = TPC * TILE // rows_n
    pairs = MAXT * MAXT
    steps = jnp.arange(MAXT, dtype=jnp.int32)
    keep = jnp.maximum(pattern, jnp.eye(count, dtype=jnp.int32))
    local_keep = lax.dynamic_slice(keep, (me_row * row_tiles, me_col * TPC), (row_tiles, TPC))
    full_keep = jnp.repeat(jnp.repeat(local_keep, TILE, axis=0), TILE, axis=1)
    masked = jnp.where(full_keep > 0, hamiltonian, jnp.zeros_like(hamiltonian))
    blocks = (
        masked.reshape(row_tiles, TILE, TPC, TILE)
        .transpose(0, 2, 1, 3)
        .reshape(row_tiles * TPC, TILE, TILE)
    )
    live_all = steps[None, :] < orders[:, None]
    owned = (tile_lists[:, :, None] // row_tiles == me_row) & (
        tile_lists[:, None, :] // TPC == me_col
    )
    owned = owned & live_all[:, :, None] & live_all[:, None, :]
    owned = owned.reshape(devices, pairs)
    rank = jnp.cumsum(owned.astype(jnp.int32), axis=1) - 1
    local_index = (
        (tile_lists[:, :, None] - me_row * row_tiles) * TPC
        + (tile_lists[:, None, :] - me_col * TPC)
    ).reshape(devices, pairs)
    slots = []
    for slot in range(2):
        pick = owned & (rank == slot)
        found = jnp.any(pick, axis=1)
        which = jnp.sum(jnp.where(pick, local_index, 0), axis=1)
        picked = jnp.take(blocks, which, axis=0)
        slots.append(jnp.where(found[:, None, None], picked, jnp.zeros_like(picked)))
    outgoing = jnp.stack(slots, axis=1)
    arrived = lax.all_to_all(outgoing, ("row", "col"), split_axis=0, concat_axis=0, tiled=True)
    arrived = arrived.reshape(devices * 2, TILE, TILE)
    mine = lax.dynamic_index_in_dim(tile_lists, solver, 0, keepdims=False)
    order_here = lax.dynamic_index_in_dim(orders, solver, 0, keepdims=False)
    live = steps < order_here
    both = (live[:, None] & live[None, :]).reshape(pairs)
    owner = (mine[:, None] // row_tiles * cols_n + mine[None, :] // TPC).reshape(pairs)
    flat_pairs = jnp.arange(pairs, dtype=jnp.int32)
    earlier = (
        (owner[:, None] == owner[None, :])
        & both[None, :]
        & (flat_pairs[None, :] < flat_pairs[:, None])
    )
    slot_of = jnp.sum(earlier.astype(jnp.int32), axis=1)
    source = jnp.where(both, owner * 2 + slot_of, 0)
    sub = jnp.take(arrived, source, axis=0)
    sub = jnp.where(both[:, None, None], sub, jnp.zeros_like(sub))
    sub = (
        sub.reshape(MAXT, MAXT, TILE, TILE).transpose(0, 2, 1, 3).reshape(MAXT * TILE, MAXT * TILE)
    )
    live_rows = jnp.repeat(live.astype(jnp.float32), TILE)
    dens = newton_density(sub, live_rows, shift[0])
    offset = solver * width % TILE
    central = lax.dynamic_slice_in_dim(dens, offset, width, 1).astype(jnp.bfloat16)
    central = central.reshape(MAXT, TILE, width).transpose(0, 2, 1)
    home_col = solver * width // (TPC * TILE)
    groups = mine // row_tiles
    ahead = (groups[:, None] == groups[None, :]) & live[None, :] & (steps[None, :] < steps[:, None])
    place = jnp.sum(ahead.astype(jnp.int32), axis=1)
    target = groups * cols_n + home_col
    chooser = jnp.arange(devices, dtype=jnp.int32)[:, None, None] == target[None, None, :]
    chooser = (
        chooser
        & (jnp.arange(2, dtype=jnp.int32)[None, :, None] == place[None, None, :])
        & live[None, None, :]
    )
    back = jnp.einsum(
        "dki,iwt->dkwt", chooser.astype(jnp.bfloat16), central, preferred_element_type=jnp.float32
    ).astype(jnp.bfloat16)
    returned = lax.all_to_all(back, ("row", "col"), split_axis=0, concat_axis=0, tiled=True)
    returned = returned.reshape(devices * 2, width, TILE)
    homes = lax.dynamic_slice_in_dim(tile_lists, me_col * rows_n, rows_n, 0)
    home_orders = lax.dynamic_slice_in_dim(orders, me_col * rows_n, rows_n, 0)
    home_live = steps[None, :] < home_orders[:, None]
    home_groups = homes // row_tiles
    home_ahead = (
        (home_groups[:, :, None] == home_groups[:, None, :])
        & home_live[:, None, :]
        & (steps[None, None, :] < steps[None, :, None])
    )
    home_place = jnp.sum(home_ahead.astype(jnp.int32), axis=2)
    local_rows = me_row * row_tiles + jnp.arange(row_tiles, dtype=jnp.int32)
    hit = (homes[None, :, :] == local_rows[:, None, None]) & home_live[None, :, :]
    found = jnp.any(hit, axis=2)
    slot_here = jnp.sum(jnp.where(hit, home_place[None, :, :], 0), axis=2)
    sub_index = me_col * rows_n + jnp.arange(rows_n, dtype=jnp.int32)
    flat_index = jnp.where(found, sub_index[None, :] * 2 + slot_here, 0)
    pieces = jnp.take(returned, flat_index.reshape(-1), axis=0).reshape(
        row_tiles, rows_n, width, TILE
    )
    pieces = jnp.where(found[:, :, None, None], pieces, jnp.zeros_like(pieces))
    density = pieces.transpose(0, 3, 1, 2).reshape(row_tiles * TILE, rows_n * width)
    p_strip = lax.all_gather(density, "row", axis=0, tiled=True)
    part = p_strip
    hp = jnp.dot(
        lax.all_gather(masked, "col", axis=1, tiled=True), part, preferred_element_type=jnp.float32
    ).astype(jnp.bfloat16)
    q_strip = lax.all_gather(hp, "row", axis=0, tiled=True)
    part = q_strip
    php = jnp.dot(
        lax.all_gather(density, "col", axis=1, tiled=True), part, preferred_element_type=jnp.float32
    )
    return (density, php)


def solution(mesh):
    in_specs = (P("row", "col"), P(), P(), P(), P())
    out_specs = (P("row", "col"), P("row", "col"))
    return jax.shard_map(
        per_device, mesh=mesh, in_specs=in_specs, out_specs=out_specs, check_vma=False
    )
```

profile of v0, /device:TPU:0, one launch (start us, length us, event | category | flops | bytes accessed | tf_op | source)
XLA Modules:
  0.0 244.3 jit_solution(1091136820264881119)
XLA Ops:
  7.2 0.7 fusion.31
  7.9 0.7 subtract_multiply_fusion
  8.6 0.7 iota_compare_fusion.2
  10.0 0.8 fusion.42
  11.0 1.1 copy.77
  12.4 0.7 gather_fusion.2
  13.2 0.7 gather_fusion.3
  14.6 1.5 copy.81
  16.1 7.3 %all-to-all-start = ((bf16[32,2,128,128]{3,2,1,0:T(8,128)(2,1)}), bf16[32,2,128,128]{3,2,1,0:T(8,128)(2,1)S(1)}, u32[]{:S(2)}, u32[]{:S(2)}) async-start(bf16[32,2,128,128]{3,2,1,0:T(8,128)(2,1)} %copy.81), calls=%async_computation | async-start | bytes 4194304 | tf_op jit(solution)/shard_map/all_to_all | solution.py:68
  23.5 0.7 all-gather.7.cloned.1.call-update
  28.5 43.7 %all-to-all-done = bf16[32,2,128,128]{3,2,1,0:T(8,128)(2,1)S(1)} async-done(((bf16[32,2,128,128]{3,2,1,0:T(8,128)(2,1)}), bf16[32,2,128,128]{3,2,1,0:T(8,128)(2,1)S(1)}, u32[]{:S(2)}, u32[]{:S(2)}) %all-to-all-start) | async-done | bytes 2097184 | tf_op jit(solution)/shard_map/all_to_all | solution.py:68
  72.2 1.3 copy-done.1
  73.5 2.5 %gather_fusion = bf16[64,128,128]{2,1,0:T(8,128)(2,1)S(1)} fusion(bf16[64,128,128]{2,1,0:T(8,128)(2,1)} %bitcast.105, s32[1024]{0:T(1024)S(1)} %pad_clamp_fusion.1), kind=kCustom, calls=%fused_computation.2 | custom fusion | bytes 4194560 | tf_op jit(solution)/shard_map/jit(_take)/gather | solution.py:83
  76.1 2.4 convert_bitcast_fusion
  78.5 1.7 multiply_reduce_fusion
  81.5 1.8 divide_convert_fusion
  83.3 1.4 copy.83
  84.7 4.3 %copy.82 = f32[8,128,8,128]{3,2,1,0:T(8,128)} copy(f32[8,128,8,128]{3,1,2,0:T(8,128)S(1)} %copy-done) | data formatting | bytes 8388608 | tf_op jit(solution)/shard_map/convert_element_type | solution.py:14
  89.0 8.2 %fusion.9 = bf16[1024,1024]{1,0:T(8,128)(2,1)} fusion(f32[128,8,8,128]{3,2,1,0:T(8,128)} %bitcast.106, f32[]{:T(128)S(6)} %add.284, f32[1024]{0:T(1024)S(1)} %broadcast_bitcast_fusion, f32[]{:T(128)} %bitcast.98, bf16[128,8,8,128]{3,2,1,0:T(8,128)(2,1)S(1)} %bitcast.110), kind=kOutput, calls=%fused_computation.23 | convolution fusion | flops 4307550208 | bytes 8392712 | tf_op jit(solution)/shard_map/dot_general | solution.py:22
  97.1 7.5 %convolution_convert_fusion = bf16[1024,1024]{1,0:T(8,128)(2,1)S(1)} fusion(bf16[1024,1024]{1,0:T(8,128)(2,1)} %fusion.9), kind=kOutput, calls=%fused_computation.24 | convolution fusion | flops 4301258752 | bytes 4194304 | tf_op jit(solution)/shard_map/dot_general | solution.py:22
  104.7 6.6 %fusion.16 = f32[1024,1024]{1,0:T(8,128)} fusion(bf16[1024,1024]{1,0:T(8,128)(2,1)S(1)} %convolution_convert_fusion), kind=kOutput, calls=%fused_computation.31 | convolution fusion | flops 4300210176 | bytes 6291456 | tf_op jit(solution)/shard_map/dot_general | solution.py:22
  111.3 1.4 fusion.18
  113.4 1.4 copy.86
  114.8 4.1 %all-to-all-start.1 = ((bf16[32,2,64,128]{3,2,1,0:T(8,128)(2,1)}), bf16[32,2,64,128]{3,2,1,0:T(8,128)(2,1)S(1)}, u32[]{:S(2)}, u32[]{:S(2)}) async-start(bf16[32,2,64,128]{3,2,1,0:T(8,128)(2,1)} %copy.86), calls=%async_computation.1 | async-start | bytes 2097152 | tf_op jit(solution)/shard_map/all_to_all | solution.py:107
  120.2 25.0 %all-to-all-done.1 = bf16[32,2,64,128]{3,2,1,0:T(8,128)(2,1)S(1)} async-done(((bf16[32,2,64,128]{3,2,1,0:T(8,128)(2,1)}), bf16[32,2,64,128]{3,2,1,0:T(8,128)(2,1)S(1)}, u32[]{:S(2)}, u32[]{:S(2)}) %all-to-all-start.1) | async-done | bytes 1048608 | tf_op jit(solution)/shard_map/all_to_all | solution.py:107
  146.1 0.7 copy.107
  146.9 27.1 %all-gather.9.cloned.1.call-done = bf16[2048,256]{0,1:T(8,128)(2,1)} async-done(((bf16[512,256]{0,1:T(8,128)(2,1)}), bf16[2048,256]{0,1:T(8,128)(2,1)}) %all-gather.9.cloned.1.call-update) | async-done | bytes 1048592 | tf_op jit(solution)/shard_map/all_gather | solution.py:130
  174.0 3.3 %convolution_convert_fusion.2 = bf16[512,256]{1,0:T(8,128)(2,1)} fusion(bf16[512,2048]{0,1:T(8,128)(2,1)} %all-gather.7.cloned.1.call-done, bf16[2048,256]{0,1:T(8,128)(2,1)} %all-gather.9.cloned.1.call-done), kind=kOutput, calls=%fused_computation.26 | convolution fusion | flops 537001984 | bytes 3407872 | tf_op jit(solution)/shard_map/dot_general | solution.py:132
  177.9 0.8 copy.88
  178.8 26.1 %all-gather.11.cloned.1.call-done = bf16[2048,256]{1,0:T(8,128)(2,1)} async-done(((bf16[512,256]{1,0:T(8,128)(2,1)}), bf16[2048,256]{1,0:T(8,128)(2,1)}) %all-gather.11.cloned.1.call-update) | async-done | bytes 1048592 | tf_op jit(solution)/shard_map/all_gather | solution.py:135
  204.8 29.5 %all-gather.5.cloned.1.call-done = bf16[512,2048]{0,1:T(8,128)(2,1)} async-done(((bf16[512,256]{0,1:T(8,128)(2,1)}), bf16[512,2048]{0,1:T(8,128)(2,1)}) %all-gather.5.cloned.1.call-update) | async-done | bytes 2097168 | tf_op jit(solution)/shard_map/all_gather | solution.py:138
  234.3 3.4 %fusion.59 = f32[512,256]{1,0:T(8,128)} fusion(bf16[512,2048]{0,1:T(8,128)(2,1)} %all-gather.5.cloned.1.call-done, bf16[2048,256]{1,0:T(8,128)(2,1)} %all-gather.11.cloned.1.call-done), kind=kOutput, calls=%fused_computation.154 | convolution fusion | flops 536870912 | bytes 3670016 | tf_op jit(solution)/shard_map/dot_general | solution.py:137
  (83 shorter events, 9.5 us)
Async XLA Ops:
  12.1 2.3 copy-start.3
  14.6 9.6 %copy-start.5 = (s32[32]{0:T(128)S(1)}, s32[32]{0:T(128)}, u32[]{:S(2)}) copy-start(s32[32]{0:T(128)} %param.10) | copy-start | bytes 388
  14.6 11.1 %copy-start.4 = (s32[32,8]{0,1:T(8,128)S(1)}, s32[32,8]{0,1:T(8,128)}, u32[]{:S(2)}) copy-start(s32[32,8]{0,1:T(8,128)} %param.9) | copy-start | bytes 3076
  16.1 56.1 %all-to-all-start = ((bf16[32,2,128,128]{3,2,1,0:T(8,128)(2,1)}), bf16[32,2,128,128]{3,2,1,0:T(8,128)(2,1)S(1)}, u32[]{:S(2)}, u32[]{:S(2)}) async-start(bf16[32,2,128,128]{3,2,1,0:T(8,128)(2,1)} %copy.81), calls=%async_computation | async-start | bytes 4194304 | tf_op jit(solution)/shard_map/all_to_all | solution.py:68
  23.4 123.5 %all-gather.7.cloned.1.call-start = ((), (), s32[]{:S(2)}) async-start(), calls=%async_computation.3 | async-start | bytes 2359296 | tf_op jit(solution)/shard_map/all_gather | solution.py:133
  72.2 1.4 copy-start.1
  81.5 3.2 %copy-start = (f32[8,128,8,128]{3,1,2,0:T(8,128)S(1)}, f32[8,128,8,128]{3,1,2,0:T(8,128)}, u32[]{:S(2)}) copy-start(f32[8,128,8,128]{3,1,2,0:T(8,128)} %convert_bitcast_fusion) | copy-start | bytes 12582916
  114.8 30.3 %all-to-all-start.1 = ((bf16[32,2,64,128]{3,2,1,0:T(8,128)(2,1)}), bf16[32,2,64,128]{3,2,1,0:T(8,128)(2,1)S(1)}, u32[]{:S(2)}, u32[]{:S(2)}) async-start(bf16[32,2,64,128]{3,2,1,0:T(8,128)(2,1)} %copy.86), calls=%async_computation.1 | async-start | bytes 2097152 | tf_op jit(solution)/shard_map/all_to_all | solution.py:107
  118.9 55.1 %all-gather.9.cloned.1.call-start = ((), (), s32[]{:S(2)}) async-start(), calls=%async_computation.4 | async-start | bytes 1310720 | tf_op jit(solution)/shard_map/all_gather | solution.py:130
  146.8 31.1 %copy-start.2 = (bf16[32,8,4,128]{3,1,2,0:T(8,128)(2,1)S(1)}, bf16[32,8,4,128]{3,1,2,0:T(8,128)(2,1)}, u32[]{:S(2)}) copy-start(bf16[32,8,4,128]{3,1,2,0:T(8,128)(2,1)} %copy.107) | copy-start | bytes 786436
  146.8 58.0 %all-gather.11.cloned.1.call-start = ((), (), s32[]{:S(2)}) async-start(), calls=%async_computation.5 | async-start | bytes 1310720 | tf_op jit(solution)/shard_map/all_gather | solution.py:135
  177.3 57.0 %all-gather.5.cloned.1.call-start = ((), (), s32[]{:S(2)}) async-start(), calls=%async_computation.2 | async-start | bytes 2359296 | tf_op jit(solution)/shard_map/all_gather | solution.py:138
Sparse Core Ops, SparseCore 0:
  26.7 35.3 all-gather.6
  146.9 26.9 all-gather.8
  177.5 27.3 all-gather.10
  207.2 27.1 all-gather.4
where the time goes:
time: 245 us; the launch traced here: 244 us
  waiting for transfers between devices  153 us (62%)
  matrix products  29.6 us (12%)
  local copies, waits for them, and re-layouts  19.7 us (8%)
  between operations  15.6 us (6%)
  other arithmetic  15.3 us (6%)
  starting transfers between devices  11.6 us (5%)
    all_to_all x1, waiting for transfers between devices, per_device(): lax.all_to_all(outgoing, ('row', 'col'), split_axis=0, concat_axis=0, til...  43.7 us
    all_gather x1, waiting for transfers between devices, per_device(): lax.all_gather(density, 'col', axis=1, tiled=True)  29.5 us
    all_gather x1, waiting for transfers between devices, per_device(): p_strip = lax.all_gather(density, 'row', axis=0, tiled=True)  27.1 us
    all_gather x1, waiting for transfers between devices, per_device(): q_strip = lax.all_gather(hp, 'row', axis=0, tiled=True)  26.1 us
    all_to_all x1, waiting for transfers between devices, per_device(): lax.all_to_all(back, ('row', 'col'), split_axis=0, concat_axis=0, tiled=T...  25 us
    dot_general x3, matrix products, newton_density(): product = jnp.dot(iterate, factor, preferred_element_type=jnp.float32)  22.3 us
    all_to_all x1, starting transfers between devices, per_device(): lax.all_to_all(outgoing, ('row', 'col'), split_axis=0, concat_axis=0, til...  7.33 us
  transfers between devices with their start and end apart: 6, of which 5 were waited for; matrix products, arithmetic and copies ran while one was open for 20% of the time, Pallas kernels for 0%

commit v1 on v0

v1 whole, which is shorter than its diff:
```python
import functools

import jax
import jax.numpy as jnp
from jax import lax
from jax.experimental import pallas as pl
from jax.experimental.pallas import tpu as pltpu
from jax.sharding import PartitionSpec as P

TILE = 128
TPC = 2
MAXT = 8
ITERS = 3
BF = jnp.bfloat16
F32 = jnp.float32
MESH = pl.DeviceIdType.MESH
SPAN = MAXT * TILE
BLOCK = 256


def eye_block(rows, cols, shift):
    r = lax.broadcasted_iota(jnp.int32, (rows, cols), 0)
    c = lax.broadcasted_iota(jnp.int32, (rows, cols), 1)
    return r == c + shift


def kernel(
    rows_n, cols_n, code, lists, orders, pattern, shift, ham,
    dens_out, php_out,
    strip, stage, arr, xa, fb, turned, cent, call, pall, pt, ptc, gall, ht, acc,
    up_s, up_r, dn_s, dn_r, aa_s, aa_r, cz_s, cz_r, pa_s, pa_r, pf_s, pf_r, ga_s, ga_r, gf_s, gf_r,
):
    me_row = lax.axis_index("row")
    me_col = lax.axis_index("col")
    high, wide = ham.shape
    row_tiles = high // TILE
    gpr = row_tiles // TPC
    groups = rows_n * gpr
    width = wide // rows_n
    pairs_n = cols_n // 2
    my_pair = me_col // 2
    parity = lax.rem(me_col, 2)
    partner = my_pair * 2 + 1 - parity
    solver = me_col * rows_n + me_row

    def send(src, dst, ss, rs, row, col):
        return pltpu.make_async_remote_copy(
            src_ref=src, dst_ref=dst, send_sem=ss, recv_sem=rs,
            device_id=(row, col), device_id_type=MESH,
        )

    barrier = pltpu.get_barrier_semaphore()
    for d in range(1, rows_n):
        pl.semaphore_signal(
            barrier, inc=1, device_id=(lax.rem(me_row + d, rows_n), me_col), device_id_type=MESH)
    for d in range(1, cols_n):
        pl.semaphore_signal(
            barrier, inc=1, device_id=(me_row, lax.rem(me_col + d, cols_n)), device_id_type=MESH)
    pl.semaphore_wait(barrier, rows_n - 1 + cols_n - 1)

    def up_copy(d):
        q = me_row - d
        src = ham if d == 0 else strip.at[jnp.maximum(q, 0)]
        return send(src, strip.at[jnp.maximum(q, 0)], up_s.at[d], up_r.at[d],
                    jnp.minimum(me_row + 1, rows_n - 1), me_col)

    def dn_copy(d):
        q = me_row + d
        src = ham if d == 0 else strip.at[jnp.minimum(q, rows_n - 1)]
        return send(src, strip.at[jnp.minimum(q, rows_n - 1)], dn_s.at[d], dn_r.at[d],
                    jnp.maximum(me_row - 1, 0), me_col)

    def sends_up(d):
        return (me_row - d >= 0) & (me_row + 1 < rows_n)

    def sends_dn(d):
        return (me_row + d < rows_n) & (me_row >= 1)

    def pick(s, g):
        return lax.rem(jnp.maximum(code[s, g], 0), 2)

    def distribute(block, q):
        def one(d, carry):
            p = lax.rem(me_col + d, cols_n)
            s = p * rows_n + me_row
            right = pick(s, me_col) == 1
            for k in range(gpr):
                g = q * gpr + k
                low = pick(s, g) == 1
                base = k * TPC * TILE
                t00 = block[base:base + TILE, 0:TILE]
                t01 = block[base:base + TILE, TILE:2 * TILE]
                t10 = block[base + TILE:base + 2 * TILE, 0:TILE]
                t11 = block[base + TILE:base + 2 * TILE, TILE:2 * TILE]
                top = jnp.where(right, t01, t00)
                bottom = jnp.where(right, t11, t10)
                stage[p, g] = jnp.where(low, bottom, top)

            @pl.when(d > 0)
            def _():
                send(stage.at[p, pl.ds(q * gpr, gpr)], arr.at[me_col, pl.ds(q * gpr, gpr)],
                     aa_s.at[q, p], aa_r.at[q, me_col], me_row, p).start()

            @pl.when(d == 0)
            def _():
                for k in range(gpr):
                    arr[me_col, q * gpr + k] = stage[me_col, q * gpr + k]
            return carry
        lax.fori_loop(0, cols_n, one, 0)

    def turn(block, q):
        for a in range(row_tiles):
            for b in range(TPC):
                ga = q * row_tiles + a
                gb = me_col * TPC + b
                keep = (pattern[ga, gb] == 1) | (ga == gb)
                t = block[a * TILE:(a + 1) * TILE, b * TILE:(b + 1) * TILE]
                t = jnp.where(keep, t, jnp.zeros_like(t))
                ht[q * gpr + a // TPC, b * TILE:(b + 1) * TILE,
                   (a % TPC) * TILE:(a % TPC + 1) * TILE] = t.T

    @pl.when(sends_up(0))
    def _():
        up_copy(0).start()

    @pl.when(sends_dn(0))
    def _():
        dn_copy(0).start()

    distribute(ham, me_row)
    for d in range(rows_n - 1):
        @pl.when(me_row - 1 - d >= 0)
        def _():
            up_copy(d).wait_recv()

            @pl.when(sends_up(d + 1))
            def _():
                up_copy(d + 1).start()
            distribute(strip.at[jnp.maximum(me_row - 1 - d, 0)], jnp.maximum(me_row - 1 - d, 0))

        @pl.when(me_row + 1 + d < rows_n)
        def _():
            dn_copy(d).wait_recv()

            @pl.when(sends_dn(d + 1))
            def _():
                dn_copy(d + 1).start()
            q = jnp.minimum(me_row + 1 + d, rows_n - 1)
            distribute(strip.at[q], q)

    turn(ham, me_row)

    def turn_other(d, carry):
        q = lax.rem(me_row + d, rows_n)
        turn(strip.at[q], q)
        return carry
    lax.fori_loop(1, rows_n, turn_other, 0)

    def wait_all(d, carry):
        p = lax.rem(me_col + d, cols_n)

        def inner(q, c):
            send(stage.at[p, pl.ds(q * gpr, gpr)], arr.at[p, pl.ds(q * gpr, gpr)],
                 aa_s.at[q, p], aa_r.at[q, p], me_row, p).wait()
            return c
        return lax.fori_loop(0, rows_n, inner, carry)
    lax.fori_loop(1, cols_n, wait_all, 0)

    potential = shift[0]
    order = orders[solver]
    eye = eye_block(TILE, TILE, 0)
    biggest = jnp.zeros((TILE, 1), F32)

    def build(i, most):
        ti = lists[solver, i]
        sums = jnp.zeros((TILE, TILE), F32)
        for j in range(MAXT):
            tj = lists[solver, j]
            keep = (i < order) & (j < order) & ((pattern[ti, tj] == 1) | (i == j))
            t = arr[tj // TPC, ti // TPC]
            t = jnp.where(keep, t, jnp.zeros_like(t))
            xa[pl.ds(pl.multiple_of(i * TILE, TILE), TILE), j * TILE:(j + 1) * TILE] = t
            v = t.astype(F32)
            move = jnp.where((i == j) & (i < order), potential, 0.0)
            v = v - jnp.where(eye, move, 0.0)
            sums += v * v
        return jnp.maximum(most, jnp.sum(sums, axis=1, keepdims=True))
    biggest = lax.fori_loop(0, MAXT, build, biggest)
    top = jnp.max(biggest, axis=0, keepdims=True)
    scale = jnp.abs(potential) + 2.0 * jnp.sqrt(top + 1e-06)
    inverse = 1.0 / scale

    def norm(i, carry):
        rows = pl.ds(pl.multiple_of(i * TILE, TILE), TILE)
        v = xa[rows, :].astype(F32)
        hit = eye_block(TILE, SPAN, 0 - i * TILE)
        move = jnp.where(i < order, potential, 0.0)
        v = v - jnp.where(hit, move, 0.0)
        xa[rows, :] = (v * inverse).astype(BF)
        return carry
    lax.fori_loop(0, MAXT, norm, 0)

    x, f = xa, fb
    for step in range(ITERS - 1):
        y = turned

        def square(n, carry):
            cols = pl.ds(pl.multiple_of(n * BLOCK, BLOCK), BLOCK)
            q = jnp.dot(x[...], x[:, cols], preferred_element_type=F32)
            hit = eye_block(SPAN, BLOCK, n * BLOCK)
            f[:, cols] = (jnp.where(hit, 1.5, 0.0) - 0.5 * q).astype(BF)
            return carry
        lax.fori_loop(0, SPAN // BLOCK, square, 0)

        def times(n, carry):
            cols = pl.ds(pl.multiple_of(n * BLOCK, BLOCK), BLOCK)
            y[:, cols] = jnp.dot(x[...], f[:, cols], preferred_element_type=F32).astype(BF)
            return carry
        lax.fori_loop(0, SPAN // BLOCK, times, 0)
        x, turned = y, x
    q = jnp.dot(x[...], x[:, 0:TILE], preferred_element_type=F32)
    hit = eye_block(SPAN, TILE, 0)
    f[:, 0:TILE] = (jnp.where(hit, 1.5, 0.0) - 0.5 * q).astype(BF)
    y3 = jnp.dot(x[...], f[:, 0:TILE], preferred_element_type=F32)
    dens = (0.5 * (jnp.where(hit, 1.0, 0.0) - y3)).astype(BF)
    for i in range(MAXT):
        cent[i] = dens[i * TILE:(i + 1) * TILE, :].T

    offset = pl.multiple_of(lax.rem(solver * width, TILE), width)
    my_rows = pl.ds(pl.multiple_of(me_row * width, width), width)

    def place(g, carry):
        where = code[solver, g]
        t = cent[jnp.maximum(where, 0) // 2, pl.ds(offset, width), :]
        call[g, my_rows, :] = jnp.where(where >= 0, t, jnp.zeros_like(t))
        return carry
    lax.fori_loop(0, groups, place, 0)

    def cz_copy(e, d):
        to = lax.rem(me_row + d, rows_n)
        part = lax.rem(me_row + d + e, rows_n)
        part_ref = call.at[pl.ds(part * gpr, gpr), my_rows, :]
        return send(part_ref, part_ref, cz_s.at[e, d], cz_r.at[e, d], to, me_col)

    for e in range(rows_n):
        for d in range(1, rows_n):
            cz_copy(e, d).start()
    for d in range(1, rows_n):
        cz_copy(0, d).wait_recv()

    mine = call.at[pl.ds(me_row * gpr, gpr)]

    def gather(src, buf, s1, r1, s2, r2):
        for d in range(1, pairs_n):
            p = lax.rem(my_pair + d, pairs_n) * 2 + parity
            send(src, buf.at[me_col], s1.at[d], r1.at[d], me_row, p).start()
        send(src, buf.at[me_col], s2.at[0], r2.at[0], me_row, partner).start()

    def arrive(buf, s1, r1, s2, r2, d):
        p = lax.rem(my_pair + pairs_n - d, pairs_n) * 2 + parity
        ref = buf.at[p]
        send(ref, ref, s1.at[d], r1.at[d], me_row, p).wait_recv()
        send(ref, ref, s2.at[d], r2.at[d], me_row, partner).start()
        return p

    def arrive2(buf, s2, r2, d):
        p = lax.rem(my_pair + pairs_n - d, pairs_n) * 2 + (1 - parity)
        ref = buf.at[p]
        send(ref, ref, s2.at[d], r2.at[d], me_row, partner).wait_recv()
        return p

    def drain(src, buf, s1, r1, s2, r2):
        for d in range(pairs_n):
            if d:
                send(src, buf.at[me_col], s1.at[d], r1.at[d], me_row, partner).wait_send()
            send(src, buf.at[me_col], s2.at[d], r2.at[d], me_row, partner).wait_send()

    gather(mine, pall, pa_s, pa_r, pf_s, pf_r)

    def spread(src, c):
        for q in range(rows_n):
            s = c * rows_n + q
            for t in range(row_tiles):
                cd = code[s, me_row * gpr + t // TPC]
                v = src[t // TPC, q * width:(q + 1) * width, :]
                ok = (cd >= 0) & (lax.rem(jnp.maximum(cd, 0), 2) == t % TPC)
                pt[q * width:(q + 1) * width, t * TILE:(t + 1) * TILE] = jnp.where(
                    ok, v, jnp.zeros_like(v))

    def term(src, c, first=False):
        spread(src, c)
        v = jnp.dot(ht[c], pt[...], preferred_element_type=F32)
        if first:
            acc[...] = v
        else:
            acc[...] += v

    term(mine, me_col, True)
    dens_out[...] = pt[...].T
    for d in range(1, pairs_n):
        p = arrive(pall, pa_s, pa_r, pf_s, pf_r, d)
        term(pall.at[p], p)
    for d in range(pairs_n):
        p = arrive2(pall, pf_s, pf_r, d)
        term(pall.at[p], p)
    gall[me_col] = acc[...].astype(BF)
    own = gall.at[me_col]
    gather(own, gall, ga_s, ga_r, gf_s, gf_r)

    for e in range(1, rows_n):
        for d in range(1, rows_n):
            cz_copy(e, d).wait_recv()
    for q in range(rows_n):
        s = me_col * rows_n + q
        for g in range(groups):
            cd = code[s, g]
            v = call[g, q * width:(q + 1) * width, :]
            for h in range(TPC):
                ok = (cd >= 0) & (lax.rem(jnp.maximum(cd, 0), 2) == h)
                ptc[g, q * width:(q + 1) * width,
                    h * TILE:(h + 1) * TILE] = jnp.where(ok, v, jnp.zeros_like(v))

    acc[...] = jnp.dot(ptc[me_col], own[...], preferred_element_type=F32)
    for d in range(1, pairs_n):
        p = arrive(gall, ga_s, ga_r, gf_s, gf_r, d)
        acc[...] += jnp.dot(ptc[p], gall[p], preferred_element_type=F32)
    for d in range(pairs_n):
        p = arrive2(gall, gf_s, gf_r, d)
        acc[...] += jnp.dot(ptc[p], gall[p], preferred_element_type=F32)
    php_out[...] = acc[...].T

    drain(mine, pall, pa_s, pa_r, pf_s, pf_r)
    drain(own, gall, ga_s, ga_r, gf_s, gf_r)
    for e in range(rows_n):
        for d in range(1, rows_n):
            cz_copy(e, d).wait_send()
    for d in range(rows_n):
        @pl.when(sends_up(d))
        def _():
            up_copy(d).wait_send()

        @pl.when(sends_dn(d))
        def _():
            dn_copy(d).wait_send()


def per_device(hamiltonian, pattern, tile_lists, orders, shift):
    rows_n = lax.axis_size("row")
    cols_n = lax.axis_size("col")
    high, wide = hamiltonian.shape
    groups = pattern.shape[0] // TPC
    gpr = high // TILE // TPC
    width = wide // rows_n
    pairs_n = cols_n // 2
    steps = jnp.arange(MAXT, dtype=jnp.int32)
    g = jnp.arange(groups, dtype=jnp.int32)
    hit = (tile_lists[:, None, :] // TPC == g[None, :, None]) & (
        steps[None, None, :] < orders[:, None, None])
    code = jnp.max(
        jnp.where(hit, steps[None, None, :] * TPC + tile_lists[:, None, :] % TPC, -1), axis=2)
    dma = pltpu.SemaphoreType.DMA
    smem = pl.BlockSpec(memory_space=pltpu.SMEM)
    vmem = pl.BlockSpec(memory_space=pltpu.VMEM)
    return pl.pallas_call(
        functools.partial(kernel, rows_n, cols_n),
        out_shape=(
            jax.ShapeDtypeStruct((high, wide), BF),
            jax.ShapeDtypeStruct((high, wide), F32),
        ),
        in_specs=[smem] * 5 + [vmem],
        out_specs=(vmem, vmem),
        scratch_shapes=[
            pltpu.VMEM((rows_n, high, wide), BF),
            pltpu.VMEM((cols_n, groups, TILE, TILE), BF),
            pltpu.VMEM((cols_n, groups, TILE, TILE), BF),
            pltpu.VMEM((SPAN, SPAN), BF),
            pltpu.VMEM((SPAN, SPAN), BF),
            pltpu.VMEM((SPAN, SPAN), BF),
            pltpu.VMEM((MAXT, TILE, TILE), BF),
            pltpu.VMEM((groups, wide, TILE), BF),
            pltpu.VMEM((cols_n, gpr, wide, TILE), BF),
            pltpu.VMEM((wide, high), BF),
            pltpu.VMEM((groups, wide, TPC * TILE), BF),
            pltpu.VMEM((cols_n, wide, high), BF),
            pltpu.VMEM((groups, wide, TPC * TILE), BF),
            pltpu.VMEM((wide, high), F32),
            dma((rows_n,)), dma((rows_n,)), dma((rows_n,)), dma((rows_n,)),
            dma((rows_n, cols_n)), dma((rows_n, cols_n)),
            dma((rows_n, rows_n)), dma((rows_n, rows_n)),
            dma((pairs_n,)), dma((pairs_n,)), dma((pairs_n,)), dma((pairs_n,)),
            dma((pairs_n,)), dma((pairs_n,)), dma((pairs_n,)), dma((pairs_n,)),
        ],
        compiler_params=pltpu.CompilerParams(
            collective_id=0, has_side_effects=True, vmem_limit_bytes=60000000),
    )(code, tile_lists, orders, pattern, shift, hamiltonian)


def solution(mesh):
    in_specs = (P("row", "col"), P(), P(), P(), P())
    out_specs = (P("row", "col"), P("row", "col"))
    return jax.shard_map(
        per_device, mesh=mesh, in_specs=in_specs, out_specs=out_specs, check_vma=False
    )
```

time: 245 us -> 85.9 us (0.35)
  waiting for transfers between devices: 153 us -> 0 us
  Pallas kernels: 0 us -> 79.2 us
  matrix products: 29.6 us -> 0 us
  local copies, waits for them, and re-layouts: 19.7 us -> 3.89 us
  other arithmetic: 15.3 us -> 0.76 us
  between operations: 15.6 us -> 1.33 us
  starting transfers between devices: 11.6 us -> 0 us
    all_gather x4 -> x0, waiting for transfers between devices: 82.7 us -> none  [the longest x1 29.5 us: per_device(): lax.all_gather(density, 'col', axis=1, tiled=True)]
    pallas_call x0 -> x1, Pallas kernels: none -> 79.2 us  [per_device(): pl.pallas_call(functools.partial(kernel, rows_n, cols_n), out_shape=(jax....]
    all_to_all x2 -> x0, waiting for transfers between devices: 68.7 us -> none  [the longest x1 43.7 us: per_device(): lax.all_to_all(outgoing, ('row', 'col'), split_axis=0, concat_axis=0, til...]
    dot_general x6 -> x0, matrix products: 29.6 us -> none  [the longest x3 22.3 us: newton_density(): product = jnp.dot(iterate, factor, preferred_element_type=jnp.float32)]
    all_to_all x2 -> x0, starting transfers between devices: 11.4 us -> none  [the longest x1 7.33 us: per_device(): lax.all_to_all(outgoing, ('row', 'col'), split_axis=0, concat_axis=0, til...]
    convert_element_type x4 -> x0, local copies, waits for them, and re-layouts: 7.13 us -> none  [the longest x1 4.3 us: newton_density(): shifted = sub.astype(jnp.float32) - potential * eye * live_rows[None, :]]
    convert_element_type x5 -> x0, other arithmetic: 6.19 us -> none  [the longest x1 2.37 us: newton_density(): shifted = sub.astype(jnp.float32) - potential * eye * live_rows[None, :]]
    gather x4 -> x0, local copies, waits for them, and re-layouts: 4.63 us -> none  [the longest x1 2.54 us: per_device(): sub = jnp.take(arrived, source, axis=0)]
  transfers between devices with their start and end apart: 6 -> 0, of which waited for: 5 -> 0; matrix products, arithmetic and copies ran while one was open for 20% -> 0% of each run, Pallas kernels for 0% -> 0%
where the time goes in v1:
time: 85.9 us; the launch traced here: 85.2 us
  Pallas kernels  79.2 us (92%)
  local copies, waits for them, and re-layouts  3.89 us (5%)
  between operations  1.33 us (2%)
    pallas_call x1, Pallas kernels, per_device(): pl.pallas_call(functools.partial(kernel, rows_n, cols_n), out_shape=(jax....  79.2 us
    unnamed x7, local copies, waits for them, and re-layouts  3.21 us

profile of v1, /device:TPU:0, one launch (start us, length us, event | category | flops | bytes accessed | tf_op | source)
XLA Modules:
  0.0 85.2 jit_solution(10724257066709159722)
XLA Ops:
  0.6 0.0 copy-start.1
  1.3 0.7 iota_compare_fusion.1
  2.0 0.0 copy-done.1
  2.0 0.1 add_select_fusion.1
  2.1 0.7 copy.10.code
  2.8 0.7 copy.11.lists
  3.4 79.2 %shard_map.68 = (bf16[512,256]{1,0:T(8,128)(2,1)}, f32[512,256]{1,0:T(8,128)}) custom-call(s32[32,8]{1,0:T(8,128)} %copy.10.code, s32[32,8]{1,0:T(8,128)} %copy.11.lists, s32[32]{0:T(128)} %orders.1, s32[16,16]{1,0:T(8,128)} %pattern.1, f32[1]{0:T(128)S(6)} %copy.14.shift, bf16[512,256]{1,0:T(8,128)(2,1)} %ham.1), custom_call_target="tpu_custom_call" | custom-call | tf_op jit(solution)/shard_map/pallas_call | solution.py:364
  82.7 0.0 copy-start
  82.7 1.7 %copy.15 = bf16[512,256]{1,0:T(8,128)(2,1)} copy(bf16[512,256]{1,0:T(8,128)(2,1)} %get-tuple-element.6) | data formatting | bytes 524288
  84.4 0.0 copy-done
  84.4 0.8 copy.16
  (2 shorter events, 0.0 us)
Async XLA Ops:
  0.6 1.3 %copy-start.1 = (s32[32,8]{0,1:T(8,128)S(1)}, s32[32,8]{0,1:T(8,128)}, u32[]{:S(2)}) copy-start(s32[32,8]{0,1:T(8,128)} %param.7) | copy-start | bytes 3076
  82.7 1.7 %copy-start = (f32[512,256]{1,0:T(8,128)S(1)}, f32[512,256]{1,0:T(8,128)}, u32[]{:S(2)}) copy-start(f32[512,256]{1,0:T(8,128)} %get-tuple-element.7) | copy-start | bytes 1572868

commit v2 on v1

--- a/solution.py
+++ b/solution.py
@@ -28,7 +28,7 @@
     rows_n, cols_n, code, lists, orders, pattern, shift, ham,
     dens_out, php_out,
     strip, stage, arr, xa, fb, turned, cent, call, pall, pt, ptc, gall, ht, acc,
-    up_s, up_r, dn_s, dn_r, aa_s, aa_r, cz_s, cz_r, pa_s, pa_r, pf_s, pf_r, ga_s, ga_r, gf_s, gf_r,
+    up_s, up_r, dn_s, dn_r, uq_s, uq_r, dq_s, dq_r, bz_s, bz_r, aa_s, aa_r, cz_s, cz_r, pa_s, pa_r, pf_s, pf_r, ga_s, ga_r, gf_s, gf_r,
 ):
     me_row = lax.axis_index("row")
     me_col = lax.axis_index("col")
@@ -58,134 +58,179 @@
             barrier, inc=1, device_id=(me_row, lax.rem(me_col + d, cols_n)), device_id_type=MESH)
     pl.semaphore_wait(barrier, rows_n - 1 + cols_n - 1)
 
-    def up_copy(d):
-        q = me_row - d
-        src = ham if d == 0 else strip.at[jnp.maximum(q, 0)]
-        return send(src, strip.at[jnp.maximum(q, 0)], up_s.at[d], up_r.at[d],
-                    jnp.minimum(me_row + 1, rows_n - 1), me_col)
-
-    def dn_copy(d):
-        q = me_row + d
-        src = ham if d == 0 else strip.at[jnp.minimum(q, rows_n - 1)]
-        return send(src, strip.at[jnp.minimum(q, rows_n - 1)], dn_s.at[d], dn_r.at[d],
-                    jnp.maximum(me_row - 1, 0), me_col)
-
-    def sends_up(d):
-        return (me_row - d >= 0) & (me_row + 1 < rows_n)
-
-    def sends_dn(d):
-        return (me_row + d < rows_n) & (me_row >= 1)
+    half_rows = TPC * TILE
+
+    def first(q):
+        return jnp.where(q == my_pair, 0, jnp.where(q < my_pair, parity, 1 - parity))
+
+    def rows_of(half):
+        return pl.ds(pl.multiple_of(half * half_rows, half_rows), half_rows)
+
+    def chain(d, up, other):
+        q = jnp.clip(me_row - d if up else me_row + d, 0, rows_n - 1)
+        to = jnp.clip(me_row + 1 if up else me_row - 1, 0, rows_n - 1)
+        half = 1 - first(q) if other else first(q)
+        rows = rows_of(half)
+        src = ham.at[rows] if d == 0 else strip.at[q, rows]
+        ss, rs = ((uq_s, uq_r) if up else (dq_s, dq_r)) if other else (
+            (up_s, up_r) if up else (dn_s, dn_r))
+        return send(src, strip.at[q, rows], ss.at[d], rs.at[d], to, me_col)
+
+    def source(d, up):
+        return me_row - d if up else me_row + d
+
+    def sends(d, up):
+        q = source(d, up)
+        return (q >= 0) & (me_row + 1 < rows_n) if up else (q < rows_n) & (me_row >= 1)
+
+    def start_chain(d, up):
+        @pl.when(sends(d, up))
+        def _():
+            chain(d, up, False).start()
+
+        @pl.when(sends(d, up) & (source(d, up) == my_pair))
+        def _():
+            chain(d, up, True).start()
+
+    def rest(d):
+        rows = rows_of(1 - first(me_row))
+        return send(ham.at[rows], strip.at[me_row, rows], bz_s.at[d], bz_r.at[d],
+                    lax.rem(me_row + d, rows_n), me_col)
+
+    def rest_in(d):
+        q = lax.rem(me_row + rows_n - d, rows_n)
+        ref = strip.at[q, rows_of(1 - first(q))]
+        return q, send(ref, ref, bz_s.at[d], bz_r.at[d], lax.rem(me_row + d, rows_n), me_col)
 
     def pick(s, g):
         return lax.rem(jnp.maximum(code[s, g], 0), 2)
 
-    def distribute(block, q):
+    def distribute(block, q, half, slot):
+        g = q * gpr + half
+        base = half * half_rows
+
         def one(d, carry):
             p = lax.rem(me_col + d, cols_n)
             s = p * rows_n + me_row
             right = pick(s, me_col) == 1
-            for k in range(gpr):
-                g = q * gpr + k
-                low = pick(s, g) == 1
-                base = k * TPC * TILE
-                t00 = block[base:base + TILE, 0:TILE]
-                t01 = block[base:base + TILE, TILE:2 * TILE]
-                t10 = block[base + TILE:base + 2 * TILE, 0:TILE]
-                t11 = block[base + TILE:base + 2 * TILE, TILE:2 * TILE]
-                top = jnp.where(right, t01, t00)
-                bottom = jnp.where(right, t11, t10)
-                stage[p, g] = jnp.where(low, bottom, top)
+            low = pick(s, g) == 1
+            above = pl.ds(pl.multiple_of(base, TILE), TILE)
+            below = pl.ds(pl.multiple_of(base + TILE, TILE), TILE)
+            top = jnp.where(right, block[above, TILE:2 * TILE], block[above, 0:TILE])
+            bottom = jnp.where(right, block[below, TILE:2 * TILE], block[below, 0:TILE])
+            tile = jnp.where(low, bottom, top)
 
             @pl.when(d > 0)
             def _():
-                send(stage.at[p, pl.ds(q * gpr, gpr)], arr.at[me_col, pl.ds(q * gpr, gpr)],
-                     aa_s.at[q, p], aa_r.at[q, me_col], me_row, p).start()
+                stage[p, slot] = tile
+                send(stage.at[p, slot], arr.at[me_col, slot],
+                     aa_s.at[slot, p], aa_r.at[slot, me_col], me_row, p).start()
 
             @pl.when(d == 0)
             def _():
-                for k in range(gpr):
-                    arr[me_col, q * gpr + k] = stage[me_col, q * gpr + k]
+                arr[me_col, slot] = tile
             return carry
         lax.fori_loop(0, cols_n, one, 0)
 
-    def turn(block, q):
-        for a in range(row_tiles):
+    def deal(block, q):
+        distribute(block, q, first(q), q)
+
+        @pl.when(q == my_pair)
+        def _():
+            distribute(block, q, 1 - first(q), rows_n)
+
+    def turn(block, q, half):
+        for a in range(TPC):
             for b in range(TPC):
-                ga = q * row_tiles + a
+                ga = q * row_tiles + half * TPC + a
                 gb = me_col * TPC + b
                 keep = (pattern[ga, gb] == 1) | (ga == gb)
-                t = block[a * TILE:(a + 1) * TILE, b * TILE:(b + 1) * TILE]
+                rows = pl.ds(pl.multiple_of(half * half_rows + a * TILE, TILE), TILE)
+                t = block[rows, b * TILE:(b + 1) * TILE]
                 t = jnp.where(keep, t, jnp.zeros_like(t))
-                ht[q * gpr + a // TPC, b * TILE:(b + 1) * TILE,
-                   (a % TPC) * TILE:(a % TPC + 1) * TILE] = t.T
-
-    @pl.when(sends_up(0))
+                ht[q * gpr + half, b * TILE:(b + 1) * TILE, a * TILE:(a + 1) * TILE] = t.T
+
+    start_chain(0, True)
+    start_chain(0, False)
+    deal(ham, me_row)
+    for d in range(rows_n - 1):
+        for up in (True, False):
+            q = source(d + 1, up)
+            here = (q >= 0) & (q < rows_n)
+
+            @pl.when(here)
+            def _():
+                chain(d, up, False).wait_recv()
+
+            @pl.when(here & (q == my_pair))
+            def _():
+                chain(d, up, True).wait_recv()
+
+            @pl.when(here)
+            def _():
+                start_chain(d + 1, up)
+                at = jnp.clip(q, 0, rows_n - 1)
+                deal(strip.at[at], at)
+
+    @pl.when(me_row != my_pair)
     def _():
-        up_copy(0).start()
-
-    @pl.when(sends_dn(0))
-    def _():
-        dn_copy(0).start()
-
-    distribute(ham, me_row)
-    for d in range(rows_n - 1):
-        @pl.when(me_row - 1 - d >= 0)
-        def _():
-            up_copy(d).wait_recv()
-
-            @pl.when(sends_up(d + 1))
-            def _():
-                up_copy(d + 1).start()
-            distribute(strip.at[jnp.maximum(me_row - 1 - d, 0)], jnp.maximum(me_row - 1 - d, 0))
-
-        @pl.when(me_row + 1 + d < rows_n)
-        def _():
-            dn_copy(d).wait_recv()
-
-            @pl.when(sends_dn(d + 1))
-            def _():
-                dn_copy(d + 1).start()
-            q = jnp.minimum(me_row + 1 + d, rows_n - 1)
-            distribute(strip.at[q], q)
-
-    turn(ham, me_row)
+        for d in range(1, rows_n):
+            rest(d).start()
+
+    turn(ham, me_row, 0)
+    turn(ham, me_row, 1)
 
     def turn_other(d, carry):
         q = lax.rem(me_row + d, rows_n)
-        turn(strip.at[q], q)
+        turn(strip.at[q], q, first(q))
         return carry
     lax.fori_loop(1, rows_n, turn_other, 0)
 
     def wait_all(d, carry):
         p = lax.rem(me_col + d, cols_n)
 
-        def inner(q, c):
-            send(stage.at[p, pl.ds(q * gpr, gpr)], arr.at[p, pl.ds(q * gpr, gpr)],
-                 aa_s.at[q, p], aa_r.at[q, p], me_row, p).wait()
+        def inner(slot, c):
+            send(stage.at[p, slot], arr.at[p, slot],
+                 aa_s.at[slot, p], aa_r.at[slot, p], me_row, p).wait()
             return c
-        return lax.fori_loop(0, rows_n, inner, carry)
+        return lax.fori_loop(0, rows_n + 1, inner, carry)
     lax.fori_loop(1, cols_n, wait_all, 0)
 
     potential = shift[0]
     order = orders[solver]
-    eye = eye_block(TILE, TILE, 0)
-    biggest = jnp.zeros((TILE, 1), F32)
-
-    def build(i, most):
+
+    def slot_of(g, h):
+        return jnp.where((g // TPC == h // TPC) & (lax.rem(g, TPC) == 1), rows_n, g // TPC)
+
+    for i in range(MAXT):
         ti = lists[solver, i]
-        sums = jnp.zeros((TILE, TILE), F32)
-        for j in range(MAXT):
+        gi = ti // TPC
+        for j in range(i, MAXT):
             tj = lists[solver, j]
-            keep = (i < order) & (j < order) & ((pattern[ti, tj] == 1) | (i == j))
-            t = arr[tj // TPC, ti // TPC]
-            t = jnp.where(keep, t, jnp.zeros_like(t))
-            xa[pl.ds(pl.multiple_of(i * TILE, TILE), TILE), j * TILE:(j + 1) * TILE] = t
-            v = t.astype(F32)
-            move = jnp.where((i == j) & (i < order), potential, 0.0)
-            v = v - jnp.where(eye, move, 0.0)
-            sums += v * v
-        return jnp.maximum(most, jnp.sum(sums, axis=1, keepdims=True))
-    biggest = lax.fori_loop(0, MAXT, build, biggest)
+            gj = tj // TPC
+            keep = (i < order) & (j < order)
+            here = slice(i * TILE, (i + 1) * TILE)
+            there = slice(j * TILE, (j + 1) * TILE)
+            if i == j:
+                t = arr[gi, slot_of(gi, gi)]
+                xa[here, here] = jnp.where(keep, t, jnp.zeros_like(t))
+                continue
+            keep = keep & (pattern[ti, tj] == 1)
+            even = lax.rem(gi + gj, 2) == 0
+            ri, rj = gi // TPC, gj // TPC
+            as_is = (ri == rj) | ((ri < rj) & even) | ((ri > rj) & jnp.logical_not(even))
+            w = jnp.where(as_is, arr[gj, slot_of(gi, gj)], arr[gi, slot_of(gj, gi)])
+            w = jnp.where(keep, w, jnp.zeros_like(w))
+            wt = w.T
+            xa[here, there] = jnp.where(as_is, w, wt)
+            xa[there, here] = jnp.where(as_is, wt, w)
+
+    def squares(i, most):
+        v = xa[pl.ds(pl.multiple_of(i * TILE, TILE), TILE), :].astype(F32)
+        move = jnp.where(i < order, potential, 0.0)
+        v = v - jnp.where(eye_block(TILE, SPAN, 0 - i * TILE), move, 0.0)
+        return jnp.maximum(most, jnp.sum(v * v, axis=1, keepdims=True))
+    biggest = lax.fori_loop(0, MAXT, squares, jnp.zeros((TILE, 1), F32))
     top = jnp.max(biggest, axis=0, keepdims=True)
     scale = jnp.abs(potential) + 2.0 * jnp.sqrt(top + 1e-06)
     inverse = 1.0 / scale
@@ -245,6 +290,16 @@
     for e in range(rows_n):
         for d in range(1, rows_n):
             cz_copy(e, d).start()
+
+    def turn_rest(d):
+        q, copy = rest_in(d)
+
+        @pl.when(q != my_pair)
+        def _():
+            copy.wait_recv()
+        turn(strip.at[q], q, 1 - first(q))
+    for d in range(1, rows_n):
+        turn_rest(d)
     for d in range(1, rows_n):
         cz_copy(0, d).wait_recv()
 
@@ -335,13 +390,19 @@
         for d in range(1, rows_n):
             cz_copy(e, d).wait_send()
     for d in range(rows_n):
-        @pl.when(sends_up(d))
-        def _():
-            up_copy(d).wait_send()
-
-        @pl.when(sends_dn(d))
-        def _():
-            dn_copy(d).wait_send()
+        for up in (True, False):
+            @pl.when(sends(d, up))
+            def _():
+                chain(d, up, False).wait_send()
+
+            @pl.when(sends(d, up) & (source(d, up) == my_pair))
+            def _():
+                chain(d, up, True).wait_send()
+
+    @pl.when(me_row != my_pair)
+    def _():
+        for d in range(1, rows_n):
+            rest(d).wait_send()
 
 
 def per_device(hamiltonian, pattern, tile_lists, orders, shift):
@@ -371,8 +432,8 @@
         out_specs=(vmem, vmem),
         scratch_shapes=[
             pltpu.VMEM((rows_n, high, wide), BF),
-            pltpu.VMEM((cols_n, groups, TILE, TILE), BF),
-            pltpu.VMEM((cols_n, groups, TILE, TILE), BF),
+            pltpu.VMEM((cols_n, rows_n + 1, TILE, TILE), BF),
+            pltpu.VMEM((cols_n, rows_n + 1, TILE, TILE), BF),
             pltpu.VMEM((SPAN, SPAN), BF),
             pltpu.VMEM((SPAN, SPAN), BF),
             pltpu.VMEM((SPAN, SPAN), BF),
@@ -384,8 +445,8 @@
             pltpu.VMEM((cols_n, wide, high), BF),
             pltpu.VMEM((groups, wide, TPC * TILE), BF),
             pltpu.VMEM((wide, high), F32),
-            dma((rows_n,)), dma((rows_n,)), dma((rows_n,)), dma((rows_n,)),
-            dma((rows_n, cols_n)), dma((rows_n, cols_n)),
+            *[dma((rows_n,))] * 10,
+            dma((rows_n + 1, cols_n)), dma((rows_n + 1, cols_n)),
             dma((rows_n, rows_n)), dma((rows_n, rows_n)),
             dma((pairs_n,)), dma((pairs_n,)), dma((pairs_n,)), dma((pairs_n,)),
             dma((pairs_n,)), dma((pairs_n,)), dma((pairs_n,)), dma((pairs_n,)),

time: 85.9 us -> 89 us (1.036)
  Pallas kernels: 79.2 us -> 82.8 us
    pallas_call x1, Pallas kernels: 79.2 us -> 82.8 us  [per_device(): pl.pallas_call(functools.partial(kernel, rows_n, cols_n), out_shape=(jax....]
where the time goes in v2:
time: 89 us; the launch traced here: 88.7 us
  Pallas kernels  82.8 us (93%)
  local copies, waits for them, and re-layouts  3.89 us (4%)
  between operations  1.33 us (1%)
    pallas_call x1, Pallas kernels, per_device(): pl.pallas_call(functools.partial(kernel, rows_n, cols_n), out_shape=(jax....  82.8 us
    unnamed x7, local copies, waits for them, and re-layouts  3.21 us

profile of v2, /device:TPU:0, one launch (start us, length us, event | category | flops | bytes accessed | tf_op | source)
XLA Modules:
  0.0 88.7 jit_solution(12305756606761751741)
XLA Ops:
  0.6 0.0 copy-start.1
  1.3 0.7 iota_compare_fusion.1
  2.0 0.0 copy-done.1
  2.0 0.1 add_select_fusion.1
  2.1 0.7 copy.10.code
  2.8 0.7 copy.11.lists
  3.4 82.8 %shard_map.68 = (bf16[512,256]{1,0:T(8,128)(2,1)}, f32[512,256]{1,0:T(8,128)}) custom-call(s32[32,8]{1,0:T(8,128)} %copy.10.code, s32[32,8]{1,0:T(8,128)} %copy.11.lists, s32[32]{0:T(128)} %orders.1, s32[16,16]{1,0:T(8,128)} %pattern.1, f32[1]{0:T(128)S(6)} %copy.14.shift, bf16[512,256]{1,0:T(8,128)(2,1)} %ham.1), custom_call_target="tpu_custom_call" | custom-call | tf_op jit(solution)/shard_map/pallas_call | solution.py:425
  86.2 0.0 copy-start
  86.2 1.7 %copy.15 = bf16[512,256]{1,0:T(8,128)(2,1)} copy(bf16[512,256]{1,0:T(8,128)(2,1)} %get-tuple-element.6) | data formatting | bytes 524288
  88.0 0.0 copy-done
  88.0 0.8 copy.16
  (2 shorter events, 0.0 us)
Async XLA Ops:
  0.6 1.3 %copy-start.1 = (s32[32,8]{0,1:T(8,128)S(1)}, s32[32,8]{0,1:T(8,128)}, u32[]{:S(2)}) copy-start(s32[32,8]{0,1:T(8,128)} %param.7) | copy-start | bytes 3076
  86.2 1.7 %copy-start = (f32[512,256]{1,0:T(8,128)S(1)}, f32[512,256]{1,0:T(8,128)}, u32[]{:S(2)}) copy-start(f32[512,256]{1,0:T(8,128)} %get-tuple-element.7) | copy-start | bytes 1572868

commit v3 on v2

--- a/solution.py
+++ b/solution.py
@@ -28,7 +28,7 @@
     rows_n, cols_n, code, lists, orders, pattern, shift, ham,
     dens_out, php_out,
     strip, stage, arr, xa, fb, turned, cent, call, pall, pt, ptc, gall, ht, acc,
-    up_s, up_r, dn_s, dn_r, uq_s, uq_r, dq_s, dq_r, bz_s, bz_r, aa_s, aa_r, cz_s, cz_r, pa_s, pa_r, pf_s, pf_r, ga_s, ga_r, gf_s, gf_r,
+    az_s, az_r, bz_s, bz_r, aa_s, aa_r, cz_s, cz_r, pa_s, pa_r, pf_s, pf_r, ga_s, ga_r, gf_s, gf_r,
 ):
     me_row = lax.axis_index("row")
     me_col = lax.axis_index("col")
@@ -66,41 +66,17 @@
     def rows_of(half):
         return pl.ds(pl.multiple_of(half * half_rows, half_rows), half_rows)
 
-    def chain(d, up, other):
-        q = jnp.clip(me_row - d if up else me_row + d, 0, rows_n - 1)
-        to = jnp.clip(me_row + 1 if up else me_row - 1, 0, rows_n - 1)
-        half = 1 - first(q) if other else first(q)
-        rows = rows_of(half)
-        src = ham.at[rows] if d == 0 else strip.at[q, rows]
-        ss, rs = ((uq_s, uq_r) if up else (dq_s, dq_r)) if other else (
-            (up_s, up_r) if up else (dn_s, dn_r))
-        return send(src, strip.at[q, rows], ss.at[d], rs.at[d], to, me_col)
-
-    def source(d, up):
-        return me_row - d if up else me_row + d
-
-    def sends(d, up):
-        q = source(d, up)
-        return (q >= 0) & (me_row + 1 < rows_n) if up else (q < rows_n) & (me_row >= 1)
-
-    def start_chain(d, up):
-        @pl.when(sends(d, up))
-        def _():
-            chain(d, up, False).start()
-
-        @pl.when(sends(d, up) & (source(d, up) == my_pair))
-        def _():
-            chain(d, up, True).start()
-
-    def rest(d):
-        rows = rows_of(1 - first(me_row))
-        return send(ham.at[rows], strip.at[me_row, rows], bz_s.at[d], bz_r.at[d],
+    def piece(d, other):
+        half = 1 - first(me_row) if other else first(me_row)
+        ss, rs = (bz_s, bz_r) if other else (az_s, az_r)
+        return send(ham.at[rows_of(half)], strip.at[me_row, rows_of(half)], ss.at[d], rs.at[d],
                     lax.rem(me_row + d, rows_n), me_col)
 
-    def rest_in(d):
+    def piece_in(d, other):
         q = lax.rem(me_row + rows_n - d, rows_n)
-        ref = strip.at[q, rows_of(1 - first(q))]
-        return q, send(ref, ref, bz_s.at[d], bz_r.at[d], lax.rem(me_row + d, rows_n), me_col)
+        ref = strip.at[q, rows_of(1 - first(q) if other else first(q))]
+        ss, rs = (bz_s, bz_r) if other else (az_s, az_r)
+        return send(ref, ref, ss.at[d], rs.at[d], lax.rem(me_row + d, rows_n), me_col)
 
     def pick(s, g):
         return lax.rem(jnp.maximum(code[s, g], 0), 2)
@@ -132,13 +108,6 @@
             return carry
         lax.fori_loop(0, cols_n, one, 0)
 
-    def deal(block, q):
-        distribute(block, q, first(q), q)
-
-        @pl.when(q == my_pair)
-        def _():
-            distribute(block, q, 1 - first(q), rows_n)
-
     def turn(block, q, half):
         for a in range(TPC):
             for b in range(TPC):
@@ -150,32 +119,31 @@
                 t = jnp.where(keep, t, jnp.zeros_like(t))
                 ht[q * gpr + half, b * TILE:(b + 1) * TILE, a * TILE:(a + 1) * TILE] = t.T
 
-    start_chain(0, True)
-    start_chain(0, False)
-    deal(ham, me_row)
-    for d in range(rows_n - 1):
-        for up in (True, False):
-            q = source(d + 1, up)
-            here = (q >= 0) & (q < rows_n)
-
-            @pl.when(here)
-            def _():
-                chain(d, up, False).wait_recv()
-
-            @pl.when(here & (q == my_pair))
-            def _():
-                chain(d, up, True).wait_recv()
-
-            @pl.when(here)
-            def _():
-                start_chain(d + 1, up)
-                at = jnp.clip(q, 0, rows_n - 1)
-                deal(strip.at[at], at)
-
-    @pl.when(me_row != my_pair)
+    steps = [1, rows_n - 1] + list(range(2, rows_n - 1))
+    for d in steps:
+        piece(d, False).start()
+
+    @pl.when(me_row == my_pair)
     def _():
-        for d in range(1, rows_n):
-            rest(d).start()
+        for d in steps:
+            piece(d, True).start()
+
+    distribute(ham, me_row, first(me_row), me_row)
+
+    @pl.when(me_row == my_pair)
+    def _():
+        distribute(ham, me_row, 1 - first(me_row), rows_n)
+    for d in steps:
+        q = lax.rem(me_row + rows_n - d, rows_n)
+        piece_in(d, False).wait_recv()
+        distribute(strip.at[q], q, first(q), q)
+    for d in steps:
+        q = lax.rem(me_row + rows_n - d, rows_n)
+
+        @pl.when(q == my_pair)
+        def _():
+            piece_in(d, True).wait_recv()
+            distribute(strip.at[q], q, 1 - first(q), rows_n)
 
     turn(ham, me_row, 0)
     turn(ham, me_row, 1)
@@ -195,6 +163,11 @@
             return c
         return lax.fori_loop(0, rows_n + 1, inner, carry)
     lax.fori_loop(1, cols_n, wait_all, 0)
+
+    @pl.when(me_row != my_pair)
+    def _():
+        for d in steps:
+            piece(d, True).start()
 
     potential = shift[0]
     order = orders[solver]
@@ -291,15 +264,13 @@
         for d in range(1, rows_n):
             cz_copy(e, d).start()
 
-    def turn_rest(d):
-        q, copy = rest_in(d)
+    for d in steps:
+        q = lax.rem(me_row + rows_n - d, rows_n)
 
         @pl.when(q != my_pair)
         def _():
-            copy.wait_recv()
+            piece_in(d, True).wait_recv()
         turn(strip.at[q], q, 1 - first(q))
-    for d in range(1, rows_n):
-        turn_rest(d)
     for d in range(1, rows_n):
         cz_copy(0, d).wait_recv()
 
@@ -389,20 +360,9 @@
     for e in range(rows_n):
         for d in range(1, rows_n):
             cz_copy(e, d).wait_send()
-    for d in range(rows_n):
-        for up in (True, False):
-            @pl.when(sends(d, up))
-            def _():
-                chain(d, up, False).wait_send()
-
-            @pl.when(sends(d, up) & (source(d, up) == my_pair))
-            def _():
-                chain(d, up, True).wait_send()
-
-    @pl.when(me_row != my_pair)
-    def _():
-        for d in range(1, rows_n):
-            rest(d).wait_send()
+    for d in steps:
+        piece(d, False).wait_send()
+        piece(d, True).wait_send()
 
 
 def per_device(hamiltonian, pattern, tile_lists, orders, shift):
@@ -445,7 +405,7 @@
             pltpu.VMEM((cols_n, wide, high), BF),
             pltpu.VMEM((groups, wide, TPC * TILE), BF),
             pltpu.VMEM((wide, high), F32),
-            *[dma((rows_n,))] * 10,
+            *[dma((rows_n,))] * 4,
             dma((rows_n + 1, cols_n)), dma((rows_n + 1, cols_n)),
             dma((rows_n, rows_n)), dma((rows_n, rows_n)),
             dma((pairs_n,)), dma((pairs_n,)), dma((pairs_n,)), dma((pairs_n,)),

time: 89 us -> 84.3 us (0.947)
  Pallas kernels: 82.8 us -> 78.1 us
    pallas_call x1, Pallas kernels: 82.8 us -> 78.1 us  [per_device(): pl.pallas_call(functools.partial(kernel, rows_n, cols_n), out_shape=(jax....]
where the time goes in v3:
time: 84.3 us; the launch traced here: 84.1 us
  Pallas kernels  78.1 us (93%)
  local copies, waits for them, and re-layouts  3.89 us (5%)
  between operations  1.33 us (2%)
    pallas_call x1, Pallas kernels, per_device(): pl.pallas_call(functools.partial(kernel, rows_n, cols_n), out_shape=(jax....  78.1 us
    unnamed x7, local copies, waits for them, and re-layouts  3.21 us

profile of v3, /device:TPU:0, one launch (start us, length us, event | category | flops | bytes accessed | tf_op | source)
XLA Modules:
  0.0 84.1 jit_solution(6569180350655596521)
XLA Ops:
  0.6 0.0 copy-start.1
  1.3 0.7 iota_compare_fusion.1
  2.0 0.0 copy-done.1
  2.0 0.1 add_select_fusion.1
  2.1 0.7 copy.10.code
  2.8 0.7 copy.11.lists
  3.4 78.1 %shard_map.68 = (bf16[512,256]{1,0:T(8,128)(2,1)}, f32[512,256]{1,0:T(8,128)}) custom-call(s32[32,8]{1,0:T(8,128)} %copy.10.code, s32[32,8]{1,0:T(8,128)} %copy.11.lists, s32[32]{0:T(128)} %orders.1, s32[16,16]{1,0:T(8,128)} %pattern.1, f32[1]{0:T(128)S(6)} %copy.14.shift, bf16[512,256]{1,0:T(8,128)(2,1)} %ham.1), custom_call_target="tpu_custom_call" | custom-call | tf_op jit(solution)/shard_map/pallas_call | solution.py:385
  81.6 0.0 copy-start
  81.6 1.7 %copy.15 = bf16[512,256]{1,0:T(8,128)(2,1)} copy(bf16[512,256]{1,0:T(8,128)(2,1)} %get-tuple-element.6) | data formatting | bytes 524288
  83.3 0.0 copy-done
  83.3 0.8 copy.16
  (2 shorter events, 0.0 us)
Async XLA Ops:
  0.6 1.3 %copy-start.1 = (s32[32,8]{0,1:T(8,128)S(1)}, s32[32,8]{0,1:T(8,128)}, u32[]{:S(2)}) copy-start(s32[32,8]{0,1:T(8,128)} %param.7) | copy-start | bytes 3076
  81.6 1.7 %copy-start = (f32[512,256]{1,0:T(8,128)S(1)}, f32[512,256]{1,0:T(8,128)}, u32[]{:S(2)}) copy-start(f32[512,256]{1,0:T(8,128)} %get-tuple-element.7) | copy-start | bytes 1572868

commit v4 on v3

--- a/solution.py
+++ b/solution.py
@@ -28,7 +28,7 @@
     rows_n, cols_n, code, lists, orders, pattern, shift, ham,
     dens_out, php_out,
     strip, stage, arr, xa, fb, turned, cent, call, pall, pt, ptc, gall, ht, acc,
-    az_s, az_r, bz_s, bz_r, aa_s, aa_r, cz_s, cz_r, pa_s, pa_r, pf_s, pf_r, ga_s, ga_r, gf_s, gf_r,
+    az_s, az_r, bz_s, bz_r, aa_s, aa_r, cz_s, cz_r, pa_s, pa_r, ga_s, ga_r,
 ):
     me_row = lax.axis_index("row")
     me_col = lax.axis_index("col")
@@ -274,64 +274,88 @@
     for d in range(1, rows_n):
         cz_copy(0, d).wait_recv()
 
-    mine = call.at[pl.ds(me_row * gpr, gpr)]
-
-    def gather(src, buf, s1, r1, s2, r2):
-        for d in range(1, pairs_n):
-            p = lax.rem(my_pair + d, pairs_n) * 2 + parity
-            send(src, buf.at[me_col], s1.at[d], r1.at[d], me_row, p).start()
-        send(src, buf.at[me_col], s2.at[0], r2.at[0], me_row, partner).start()
-
-    def arrive(buf, s1, r1, s2, r2, d):
-        p = lax.rem(my_pair + pairs_n - d, pairs_n) * 2 + parity
-        ref = buf.at[p]
-        send(ref, ref, s1.at[d], r1.at[d], me_row, p).wait_recv()
-        send(ref, ref, s2.at[d], r2.at[d], me_row, partner).start()
-        return p
-
-    def arrive2(buf, s2, r2, d):
-        p = lax.rem(my_pair + pairs_n - d, pairs_n) * 2 + (1 - parity)
-        ref = buf.at[p]
-        send(ref, ref, s2.at[d], r2.at[d], me_row, partner).wait_recv()
-        return p
-
-    def drain(src, buf, s1, r1, s2, r2):
-        for d in range(pairs_n):
-            if d:
-                send(src, buf.at[me_col], s1.at[d], r1.at[d], me_row, partner).wait_send()
-            send(src, buf.at[me_col], s2.at[d], r2.at[d], me_row, partner).wait_send()
-
-    gather(mine, pall, pa_s, pa_r, pf_s, pf_r)
-
-    def spread(src, c):
+    relay = pairs_n == 4
+
+    def flip(e):
+        out, unit = 0, 1
+        while unit < pairs_n:
+            bit = lax.rem(my_pair // unit, 2)
+            out = out + unit * (1 - bit if (e // unit) % 2 else bit)
+            unit *= 2
+        return out
+
+    def net(src, buf, ss, rs, c, u, e, via):
+        return send(src, buf.at[c, u], ss.at[e, u], rs.at[e, u], me_row, flip(via) * 2 + parity)
+
+    def pass_on(src, buf, ss, rs, c, u, e):
+        return send(src, buf.at[c, u], ss.at[pairs_n + e, u], rs.at[pairs_n + e, u],
+                    me_row, partner)
+
+    def start_own(src, buf, ss, rs, u):
+        for e in range(1, 3 if relay else pairs_n):
+            net(src, buf, ss, rs, me_col, u, e, e).start()
+        pass_on(src, buf, ss, rs, me_col, u, 0).start()
+
+    def from_net(buf, ss, rs, u, e):
+        c = flip(e) * 2 + parity
+        ref = buf.at[c, u]
+        net(ref, buf, ss, rs, c, u, e, e).wait_recv()
+        if relay and (u, e) == (0, 1):
+            net(ref, buf, ss, rs, c, u, 3, 2).start()
+        if relay and (u, e) == (1, 2):
+            net(ref, buf, ss, rs, c, u, 3, 1).start()
+        pass_on(ref, buf, ss, rs, c, u, e).start()
+        return c
+
+    def from_partner(buf, ss, rs, u, e):
+        c = flip(e) * 2 + 1 - parity
+        ref = buf.at[c, u]
+        pass_on(ref, buf, ss, rs, c, u, e).wait_recv()
+        return c
+
+    def consume(buf, ss, rs, u, use):
+        last = pairs_n - 1
+        near = [from_net(buf, ss, rs, u, e) for e in range(1, last)]
+        for c in near:
+            use(c)
+        use(from_partner(buf, ss, rs, u, 0))
+        for e in range(1, last):
+            use(from_partner(buf, ss, rs, u, e))
+        use(from_net(buf, ss, rs, u, last))
+        use(from_partner(buf, ss, rs, u, last))
+
+    def drain(buf, ss, rs):
+        for u in range(gpr):
+            ref = buf.at[me_col, u]
+            for e in range(pairs_n):
+                if e:
+                    net(ref, buf, ss, rs, me_col, u, e, e).wait_send()
+                pass_on(ref, buf, ss, rs, me_col, u, e).wait_send()
+
+    for u in range(gpr):
+        start_own(call.at[me_row * gpr + u], pall, pa_s, pa_r, u)
+
+    def spread(src, c, u):
         for q in range(rows_n):
-            s = c * rows_n + q
-            for t in range(row_tiles):
-                cd = code[s, me_row * gpr + t // TPC]
-                v = src[t // TPC, q * width:(q + 1) * width, :]
-                ok = (cd >= 0) & (lax.rem(jnp.maximum(cd, 0), 2) == t % TPC)
-                pt[q * width:(q + 1) * width, t * TILE:(t + 1) * TILE] = jnp.where(
+            cd = code[c * rows_n + q, me_row * gpr + u]
+            v = src[q * width:(q + 1) * width, :]
+            for h in range(TPC):
+                ok = (cd >= 0) & (lax.rem(jnp.maximum(cd, 0), 2) == h)
+                pt[q * width:(q + 1) * width, h * TILE:(h + 1) * TILE] = jnp.where(
                     ok, v, jnp.zeros_like(v))
 
-    def term(src, c, first=False):
-        spread(src, c)
-        v = jnp.dot(ht[c], pt[...], preferred_element_type=F32)
-        if first:
-            acc[...] = v
-        else:
-            acc[...] += v
-
-    term(mine, me_col, True)
-    dens_out[...] = pt[...].T
-    for d in range(1, pairs_n):
-        p = arrive(pall, pa_s, pa_r, pf_s, pf_r, d)
-        term(pall.at[p], p)
-    for d in range(pairs_n):
-        p = arrive2(pall, pf_s, pf_r, d)
-        term(pall.at[p], p)
-    gall[me_col] = acc[...].astype(BF)
-    own = gall.at[me_col]
-    gather(own, gall, ga_s, ga_r, gf_s, gf_r)
+    for u in range(gpr):
+        rows = slice(u * half_rows, (u + 1) * half_rows)
+        spread(call.at[me_row * gpr + u], me_col, u)
+        dens_out[rows, :] = pt[...].T
+        acc[...] = jnp.dot(ht[me_col], pt[...], preferred_element_type=F32)
+
+        def term(c):
+            spread(pall.at[c, u], c, u)
+            acc[...] += jnp.dot(ht[c], pt[...], preferred_element_type=F32)
+        consume(pall, pa_s, pa_r, u, term)
+        gall[me_col, u] = acc[...].astype(BF)
+        start_own(gall.at[me_col, u], gall, ga_s, ga_r, u)
 
     for e in range(1, rows_n):
         for d in range(1, rows_n):
@@ -343,20 +367,19 @@
             v = call[g, q * width:(q + 1) * width, :]
             for h in range(TPC):
                 ok = (cd >= 0) & (lax.rem(jnp.maximum(cd, 0), 2) == h)
-                ptc[g, q * width:(q + 1) * width,
-                    h * TILE:(h + 1) * TILE] = jnp.where(ok, v, jnp.zeros_like(v))
-
-    acc[...] = jnp.dot(ptc[me_col], own[...], preferred_element_type=F32)
-    for d in range(1, pairs_n):
-        p = arrive(gall, ga_s, ga_r, gf_s, gf_r, d)
-        acc[...] += jnp.dot(ptc[p], gall[p], preferred_element_type=F32)
-    for d in range(pairs_n):
-        p = arrive2(gall, gf_s, gf_r, d)
-        acc[...] += jnp.dot(ptc[p], gall[p], preferred_element_type=F32)
-    php_out[...] = acc[...].T
-
-    drain(mine, pall, pa_s, pa_r, pf_s, pf_r)
-    drain(own, gall, ga_s, ga_r, gf_s, gf_r)
+                ptc[g, q * width:(q + 1) * width, h * TILE:(h + 1) * TILE] = jnp.where(
+                    ok, v, jnp.zeros_like(v))
+
+    for u in range(gpr):
+        acc[...] = jnp.dot(ptc[me_col], gall[me_col, u], preferred_element_type=F32)
+
+        def last_term(c):
+            acc[...] += jnp.dot(ptc[c], gall[c, u], preferred_element_type=F32)
+        consume(gall, ga_s, ga_r, u, last_term)
+        php_out[u * half_rows:(u + 1) * half_rows, :] = acc[...].T
+
+    drain(pall, pa_s, pa_r)
+    drain(gall, ga_s, ga_r)
     for e in range(rows_n):
         for d in range(1, rows_n):
             cz_copy(e, d).wait_send()
@@ -400,16 +423,15 @@
             pltpu.VMEM((MAXT, TILE, TILE), BF),
             pltpu.VMEM((groups, wide, TILE), BF),
             pltpu.VMEM((cols_n, gpr, wide, TILE), BF),
-            pltpu.VMEM((wide, high), BF),
+            pltpu.VMEM((wide, TPC * TILE), BF),
             pltpu.VMEM((groups, wide, TPC * TILE), BF),
-            pltpu.VMEM((cols_n, wide, high), BF),
+            pltpu.VMEM((cols_n, gpr, wide, TPC * TILE), BF),
             pltpu.VMEM((groups, wide, TPC * TILE), BF),
-            pltpu.VMEM((wide, high), F32),
+            pltpu.VMEM((wide, TPC * TILE), F32),
             *[dma((rows_n,))] * 4,
             dma((rows_n + 1, cols_n)), dma((rows_n + 1, cols_n)),
             dma((rows_n, rows_n)), dma((rows_n, rows_n)),
-            dma((pairs_n,)), dma((pairs_n,)), dma((pairs_n,)), dma((pairs_n,)),
-            dma((pairs_n,)), dma((pairs_n,)), dma((pairs_n,)), dma((pairs_n,)),
+            *[dma((2 * pairs_n, gpr))] * 4,
         ],
         compiler_params=pltpu.CompilerParams(
             collective_id=0, has_side_effects=True, vmem_limit_bytes=60000000),

time: 84.3 us -> 90.4 us (1.072)
  Pallas kernels: 78.1 us -> 83.8 us
    pallas_call x1, Pallas kernels: 78.1 us -> 83.8 us  [per_device(): pl.pallas_call(functools.partial(kernel, rows_n, cols_n), out_shape=(jax....]
where the time goes in v4:
time: 90.4 us; the launch traced here: 89.8 us
  Pallas kernels  83.8 us (93%)
  local copies, waits for them, and re-layouts  3.89 us (4%)
  between operations  1.33 us (1%)
    pallas_call x1, Pallas kernels, per_device(): pl.pallas_call(functools.partial(kernel, rows_n, cols_n), out_shape=(jax....  83.8 us
    unnamed x7, local copies, waits for them, and re-layouts  3.21 us

profile of v4, /device:TPU:0, one launch (start us, length us, event | category | flops | bytes accessed | tf_op | source)
XLA Modules:
  0.0 89.8 jit_solution(17175942721028327579)
XLA Ops:
  0.6 0.0 copy-start.1
  1.3 0.7 iota_compare_fusion.1
  2.0 0.0 copy-done.1
  2.0 0.1 add_select_fusion.1
  2.1 0.7 copy.10.code
  2.8 0.7 copy.11.lists
  3.4 83.8 %shard_map.68 = (bf16[512,256]{1,0:T(8,128)(2,1)}, f32[512,256]{1,0:T(8,128)}) custom-call(s32[32,8]{1,0:T(8,128)} %copy.10.code, s32[32,8]{1,0:T(8,128)} %copy.11.lists, s32[32]{0:T(128)} %orders.1, s32[16,16]{1,0:T(8,128)} %pattern.1, f32[1]{0:T(128)S(6)} %copy.14.shift, bf16[512,256]{1,0:T(8,128)(2,1)} %ham.1), custom_call_target="tpu_custom_call" | custom-call | tf_op jit(solution)/shard_map/pallas_call | solution.py:408
  87.2 0.0 copy-start
  87.2 1.7 %copy.15 = bf16[512,256]{1,0:T(8,128)(2,1)} copy(bf16[512,256]{1,0:T(8,128)(2,1)} %get-tuple-element.6) | data formatting | bytes 524288
  89.0 0.0 copy-done
  89.0 0.8 copy.16
  (2 shorter events, 0.0 us)
Async XLA Ops:
  0.6 1.3 %copy-start.1 = (s32[32,8]{0,1:T(8,128)S(1)}, s32[32,8]{0,1:T(8,128)}, u32[]{:S(2)}) copy-start(s32[32,8]{0,1:T(8,128)} %param.7) | copy-start | bytes 3076
  87.2 1.7 %copy-start = (f32[512,256]{1,0:T(8,128)S(1)}, f32[512,256]{1,0:T(8,128)}, u32[]{:S(2)}) copy-start(f32[512,256]{1,0:T(8,128)} %get-tuple-element.7) | copy-start | bytes 1572868

commit v5 on v4

--- a/solution.py
+++ b/solution.py
@@ -274,7 +274,6 @@
     for d in range(1, rows_n):
         cz_copy(0, d).wait_recv()
 
-    relay = pairs_n == 4
 
     def flip(e):
         out, unit = 0, 1
@@ -292,7 +291,7 @@
                     me_row, partner)
 
     def start_own(src, buf, ss, rs, u):
-        for e in range(1, 3 if relay else pairs_n):
+        for e in range(1, pairs_n):
             net(src, buf, ss, rs, me_col, u, e, e).start()
         pass_on(src, buf, ss, rs, me_col, u, 0).start()
 
@@ -300,10 +299,6 @@
         c = flip(e) * 2 + parity
         ref = buf.at[c, u]
         net(ref, buf, ss, rs, c, u, e, e).wait_recv()
-        if relay and (u, e) == (0, 1):
-            net(ref, buf, ss, rs, c, u, 3, 2).start()
-        if relay and (u, e) == (1, 2):
-            net(ref, buf, ss, rs, c, u, 3, 1).start()
         pass_on(ref, buf, ss, rs, c, u, e).start()
         return c
 

time: 90.4 us -> 82.6 us (0.914)
  Pallas kernels: 83.8 us -> 76.4 us
    pallas_call x1, Pallas kernels: 83.8 us -> 76.4 us  [per_device(): pl.pallas_call(functools.partial(kernel, rows_n, cols_n), out_shape=(jax....]
where the time goes in v5:
time: 82.6 us; the launch traced here: 82.4 us
  Pallas kernels  76.4 us (92%)
  local copies, waits for them, and re-layouts  3.89 us (5%)
  between operations  1.33 us (2%)
    pallas_call x1, Pallas kernels, per_device(): pl.pallas_call(functools.partial(kernel, rows_n, cols_n), out_shape=(jax....  76.4 us
    unnamed x7, local copies, waits for them, and re-layouts  3.21 us

profile of v5, /device:TPU:0, one launch (start us, length us, event | category | flops | bytes accessed | tf_op | source)
XLA Modules:
  0.0 82.4 jit_solution(6720655166825636408)
XLA Ops:
  0.6 0.0 copy-start.1
  1.3 0.7 iota_compare_fusion.1
  2.0 0.0 copy-done.1
  2.0 0.1 add_select_fusion.1
  2.1 0.7 copy.10.code
  2.8 0.7 copy.11.lists
  3.4 76.4 %shard_map.68 = (bf16[512,256]{1,0:T(8,128)(2,1)}, f32[512,256]{1,0:T(8,128)}) custom-call(s32[32,8]{1,0:T(8,128)} %copy.10.code, s32[32,8]{1,0:T(8,128)} %copy.11.lists, s32[32]{0:T(128)} %orders.1, s32[16,16]{1,0:T(8,128)} %pattern.1, f32[1]{0:T(128)S(6)} %copy.14.shift, bf16[512,256]{1,0:T(8,128)(2,1)} %ham.1), custom_call_target="tpu_custom_call" | custom-call | tf_op jit(solution)/shard_map/pallas_call | solution.py:403
  79.9 0.0 copy-start
  79.9 1.7 %copy.15 = bf16[512,256]{1,0:T(8,128)(2,1)} copy(bf16[512,256]{1,0:T(8,128)(2,1)} %get-tuple-element.6) | data formatting | bytes 524288
  81.6 0.0 copy-done
  81.6 0.8 copy.16
  (2 shorter events, 0.0 us)
Async XLA Ops:
  0.6 1.3 %copy-start.1 = (s32[32,8]{0,1:T(8,128)S(1)}, s32[32,8]{0,1:T(8,128)}, u32[]{:S(2)}) copy-start(s32[32,8]{0,1:T(8,128)} %param.7) | copy-start | bytes 3076
  79.9 1.7 %copy-start = (f32[512,256]{1,0:T(8,128)S(1)}, f32[512,256]{1,0:T(8,128)}, u32[]{:S(2)}) copy-start(f32[512,256]{1,0:T(8,128)} %get-tuple-element.7) | copy-start | bytes 1572868
